TPU v7x, 32 devices: a whole 2x2x4 slice. The times are simulated.
32 devices in a mesh: sect: 2 (over x), seq: 4 (over y, core), dp: 4 (over z).
Axes of the slice: x: 2, y: 2, z: 4, core: 2. Of those that a mesh axis runs over, the one named last changes fastest.
Arguments:
- query_tiles: bfloat16 [4, 8, 128, 2048], P('dp', None, 'sect', 'seq'), may hold values from -6 to 6
- key_tiles: bfloat16 [4, 8, 128, 2048], P('dp', None, 'sect', 'seq'), may hold values from -6 to 6
- value_tiles: bfloat16 [4, 8, 128, 2048], P('dp', None, 'sect', 'seq'), may hold values from -6 to 6
- text_keys: bfloat16 [8, 256, 2048], P(('sect', 'dp'), 'seq'), may hold values from -6 to 6
- text_values: bfloat16 [8, 256, 2048], P(('sect', 'dp'), 'seq'), may hold values from -6 to 6
- text_lengths: int32 [8], P(('sect', 'dp')), may hold values from 32 to 256, as said below
- tile_place: int32 [4], replicated, may hold values from 0 to 3, each once
Outputs:
- attended: bfloat16 [8, 512, 2048], P(('sect', 'dp'), 'seq')
Inputs may be any that keep to these rules, and one draw needn't show every extreme that they name: `tile_place`: each spatial position is held by exactly one tile slot. `text_lengths`: the live text tokens of a clip are its first rows; some clip fills all 256 slots.
All inputs are finite; a program needn't handle non-finite values.
Results may differ from a plain program's by a relative error of at most 0.0031.
Values may be sent and summed in bfloat16 or wider, within the bound.
A program may use at most 64 MiB of HBM per device.

v0:
```python
import math
import jax
import jax.numpy as jnp
from jax import lax
from jax.sharding import PartitionSpec as P

HD = 128


def attend(queries_flat, keys_video, values_video, keys_text, values_text, length):
    query_rows, head_width = queries_flat.shape
    head_count = head_width // HD
    score_scale = 1.0 / math.sqrt(HD)
    keys_video = keys_video.reshape(-1, head_count, HD)
    values_video = values_video.reshape(-1, head_count, HD)
    keys_text = keys_text.reshape(-1, head_count, HD)
    values_text = values_text.reshape(-1, head_count, HD)
    live_mask = jnp.arange(keys_text.shape[0], dtype=jnp.int32) < length
    block_rows = math.gcd(query_rows, 512)

    def one_block(query_block):
        score_video = (
            jnp.einsum("qhd,khd->hqk", query_block, keys_video, preferred_element_type=jnp.float32)
            * score_scale
        )
        score_text = (
            jnp.einsum("qhd,khd->hqk", query_block, keys_text, preferred_element_type=jnp.float32)
            * score_scale
        )
        score_text = jnp.where(live_mask[None, None, :], score_text, -jnp.inf)
        row_max = jnp.maximum(jnp.max(score_video, axis=-1), jnp.max(score_text, axis=-1))[
            ..., None
        ]
        expo_video = jnp.exp(score_video - row_max)
        expo_text = jnp.exp(score_text - row_max)
        denominators = jnp.sum(expo_video, axis=-1) + jnp.sum(expo_text, axis=-1)
        mixed = jnp.einsum(
            "hqk,khd->qhd",
            expo_video.astype(jnp.bfloat16),
            values_video,
            preferred_element_type=jnp.float32,
        )
        mixed = mixed + jnp.einsum(
            "hqk,khd->qhd",
            expo_text.astype(jnp.bfloat16),
            values_text,
            preferred_element_type=jnp.float32,
        )
        return (mixed / jnp.transpose(denominators)[:, :, None]).astype(jnp.bfloat16)

    blocks = queries_flat.reshape(query_rows // block_rows, block_rows, head_count, HD)
    return lax.map(one_block, blocks).reshape(query_rows, head_width)


def shards(query_tiles, key_tiles, value_tiles, text_keys, text_values, text_lengths, tile_place):
    tile_count = lax.axis_size("dp")
    sect_count = lax.axis_size("sect")
    part_rows = query_tiles.shape[2]
    head_width = query_tiles.shape[3]
    tile_seq = part_rows * sect_count

    def regroup(piece):
        return piece.reshape(1, sect_count, tile_count, part_rows, head_width)

    relayed = (
        lax.all_to_all(
            lax.all_to_all(regroup(query_tiles), "sect", split_axis=1, concat_axis=3, tiled=True),
            "dp",
            split_axis=2,
            concat_axis=0,
            tiled=True,
        ),
        lax.all_to_all(
            lax.all_to_all(regroup(key_tiles), "sect", split_axis=1, concat_axis=3, tiled=True),
            "dp",
            split_axis=2,
            concat_axis=0,
            tiled=True,
        ),
        lax.all_to_all(
            lax.all_to_all(regroup(value_tiles), "sect", split_axis=1, concat_axis=3, tiled=True),
            "dp",
            split_axis=2,
            concat_axis=0,
            tiled=True,
        ),
    )
    spatial_order = jnp.argsort(tile_place)
    seq_count = lax.axis_size("seq")
    tile_rows = tile_seq // seq_count

    def arrange(piece):
        grid = piece.reshape(tile_count, seq_count, tile_rows, head_width)
        placed = jnp.take(grid, spatial_order, axis=0)
        placed = jnp.transpose(placed, (1, 0, 2, 3))
        return placed.reshape(seq_count * tile_count * tile_rows, head_width)

    video_queries = arrange(relayed[0])
    video_keys = arrange(relayed[1])
    video_values = arrange(relayed[2])
    keys_text, values_text = (
        lax.all_to_all(text_keys[0], "seq", split_axis=1, concat_axis=0, tiled=True),
        lax.all_to_all(text_values[0], "seq", split_axis=1, concat_axis=0, tiled=True),
    )
    attended_heads = attend(
        video_queries, video_keys, video_values, keys_text, values_text, text_lengths[0]
    )
    attended = lax.all_to_all(attended_heads, "seq", split_axis=0, concat_axis=1, tiled=True)
    return attended[None]


def solution(mesh):
    in_specs = (
        P("dp", None, "sect", "seq"),
        P("dp", None, "sect", "seq"),
        P("dp", None, "sect", "seq"),
        P(("sect", "dp"), "seq", None),
        P(("sect", "dp"), "seq", None),
        P(("sect", "dp")),
        P(),
    )
    out_specs = P(("sect", "dp"), "seq", None)
    return jax.shard_map(shards, mesh=mesh, in_specs=in_specs, out_specs=out_specs, check_vma=False)
```

profile of v0, /device:TPU:0, one launch (start us, length us, event | category | flops | bytes accessed | tf_op | source)
XLA Modules:
  0.0 116.4 jit_solution(8662692775523040408)
XLA Ops:
  0.0 0.0 copy-start
  0.0 0.0 copy-start.1
  0.0 1.2 %all_to_all.111 = bf16[64,4,512]{2,1,0:T(4,128)(2,1)S(1)} reshape(bf16[1,64,2048]{2,1,0:T(8,128)(2,1)} %param.12) | data formatting | bytes 524288 | tf_op jit(solution)/shard_map/all_to_all | solution.py:102
  1.2 0.7 copy.57
  2.0 4.2 %all-to-all-start.6 = ((bf16[64,4,512]{2,0,1:T(8,128)(2,1)}), bf16[64,4,512]{2,0,1:T(8,128)(2,1)S(1)}, u32[]{:S(2)}, u32[]{:S(2)}) async-start(bf16[64,4,512]{2,0,1:T(8,128)(2,1)} %copy.57), calls=%async_computation.6 | async-start | bytes 524288 | tf_op jit(solution)/shard_map/all_to_all | solution.py:102
  6.2 1.1 all_to_all.114
  7.4 4.8 %all-to-all-done.6 = bf16[64,4,512]{2,0,1:T(8,128)(2,1)S(1)} async-done(((bf16[64,4,512]{2,0,1:T(8,128)(2,1)}), bf16[64,4,512]{2,0,1:T(8,128)(2,1)S(1)}, u32[]{:S(2)}, u32[]{:S(2)}) %all-to-all-start.6) | async-done | bytes 262176 | tf_op jit(solution)/shard_map/all_to_all | solution.py:102
  12.3 8.4 %all_to_all.129 = bf16[64,4,512]{2,0,1:T(8,128)(2,1)S(1)} all-to-all(bf16[64,4,512]{2,0,1:T(8,128)(2,1)S(1)} %copy.62), channel_id=1, replica_groups=mesh['sect'=2,'seq'=4,'dp'=4] {'seq'}, dimensions={1} | all-to-all | bytes 524288 | tf_op jit(solution)/shard_map/all_to_all | solution.py:103
  20.7 0.0 copy-done
  20.7 10.7 %all_to_all.130 = bf16[1,2,4,64,512]{4,3,2,0,1:T(8,128)(2,1)S(1)} all-to-all(bf16[1,2,4,64,512]{4,3,2,0,1:T(8,128)(2,1)S(1)} %bitcast.72), channel_id=1, replica_groups=mesh['sect'=2,'seq'=4,'dp'=4] {'sect'}, dimensions={1} | all-to-all | bytes 1048576 | tf_op jit(solution)/shard_map/all_to_all | solution.py:67
  31.4 0.0 copy-done.1
  31.4 9.1 %all_to_all.131 = bf16[1,2,4,64,512]{4,3,2,0,1:T(8,128)(2,1)S(1)} all-to-all(bf16[1,2,4,64,512]{4,3,2,0,1:T(8,128)(2,1)S(1)} %bitcast.73), channel_id=1, replica_groups=mesh['sect'=2,'seq'=4,'dp'=4] {'sect'}, dimensions={1} | all-to-all | bytes 1048576 | tf_op jit(solution)/shard_map/all_to_all | solution.py:74
  40.5 3.5 %all-to-all-start = ((bf16[1,2,4,64,512]{4,3,2,0,1:T(8,128)(2,1)}), bf16[1,2,4,64,512]{4,3,2,0,1:T(8,128)(2,1)S(1)}, u32[]{:S(2)}, u32[]{:S(2)}) async-start(bf16[1,2,4,64,512]{4,3,2,0,1:T(8,128)(2,1)} %bitcast.1), calls=%async_computation | async-start | bytes 1048576 | tf_op jit(solution)/shard_map/all_to_all | solution.py:81
  44.0 0.8 copy.48
  44.8 5.7 %all-to-all-done = bf16[1,2,4,64,512]{4,3,2,0,1:T(8,128)(2,1)S(1)} async-done(((bf16[1,2,4,64,512]{4,3,2,0,1:T(8,128)(2,1)}), bf16[1,2,4,64,512]{4,3,2,0,1:T(8,128)(2,1)S(1)}, u32[]{:S(2)}, u32[]{:S(2)}) %all-to-all-start) | async-done | bytes 524320 | tf_op jit(solution)/shard_map/all_to_all | solution.py:81
  50.6 5.1 %all-to-all-start.3 = ((bf16[1,1,4,128,512]{4,3,1,0,2:T(8,128)(2,1)}), bf16[1,1,4,128,512]{4,3,1,0,2:T(8,128)(2,1)S(1)}, u32[]{:S(2)}, u32[]{:S(2)}) async-start(bf16[1,1,4,128,512]{4,3,1,0,2:T(8,128)(2,1)} %bitcast.13), calls=%async_computation.3 | async-start | bytes 1048576 | tf_op jit(solution)/shard_map/all_to_all | solution.py:66
  55.7 0.0 copy-start.3
  55.7 0.8 copy.52
  56.5 10.1 %all-to-all-done.3 = bf16[1,1,4,128,512]{4,3,1,0,2:T(8,128)(2,1)S(1)} async-done(((bf16[1,1,4,128,512]{4,3,1,0,2:T(8,128)(2,1)}), bf16[1,1,4,128,512]{4,3,1,0,2:T(8,128)(2,1)S(1)}, u32[]{:S(2)}, u32[]{:S(2)}) %all-to-all-start.3) | async-done | bytes 524320 | tf_op jit(solution)/shard_map/all_to_all | solution.py:66
  66.7 3.5 %all-to-all-start.5 = ((bf16[1,1,4,128,512]{4,3,1,0,2:T(8,128)(2,1)}), bf16[1,1,4,128,512]{4,3,1,0,2:T(8,128)(2,1)S(1)}, u32[]{:S(2)}, u32[]{:S(2)}) async-start(bf16[1,1,4,128,512]{4,3,1,0,2:T(8,128)(2,1)} %bitcast.21), calls=%async_computation.5 | async-start | bytes 1048576 | tf_op jit(solution)/shard_map/all_to_all | solution.py:73
  70.2 0.8 copy.44
  71.0 10.7 %all-to-all-done.5 = bf16[1,1,4,128,512]{4,3,1,0,2:T(8,128)(2,1)S(1)} async-done(((bf16[1,1,4,128,512]{4,3,1,0,2:T(8,128)(2,1)}), bf16[1,1,4,128,512]{4,3,1,0,2:T(8,128)(2,1)S(1)}, u32[]{:S(2)}, u32[]{:S(2)}) %all-to-all-start.5) | async-done | bytes 524320 | tf_op jit(solution)/shard_map/all_to_all | solution.py:73
  81.7 3.5 %all-to-all-start.1 = ((bf16[1,1,4,128,512]{4,3,1,0,2:T(8,128)(2,1)}), bf16[1,1,4,128,512]{4,3,1,0,2:T(8,128)(2,1)S(1)}, u32[]{:S(2)}, u32[]{:S(2)}) async-start(bf16[1,1,4,128,512]{4,3,1,0,2:T(8,128)(2,1)} %bitcast.5), calls=%async_computation.1 | async-start | bytes 1048576 | tf_op jit(solution)/shard_map/all_to_all | solution.py:80
  85.8 0.0 copy-done.3
  85.9 0.7 sort.17
  86.6 0.8 reshape.75
  87.4 0.1 reshape.76
  87.5 0.6 gather_fusion.1
  88.0 0.6 gather_fusion.2
  88.6 8.7 %all-to-all-done.1 = bf16[1,1,4,128,512]{4,3,1,0,2:T(8,128)(2,1)S(1)} async-done(((bf16[1,1,4,128,512]{4,3,1,0,2:T(8,128)(2,1)}), bf16[1,1,4,128,512]{4,3,1,0,2:T(8,128)(2,1)S(1)}, u32[]{:S(2)}, u32[]{:S(2)}) %all-to-all-start.1) | async-done | bytes 524320 | tf_op jit(solution)/shard_map/all_to_all | solution.py:80
  97.3 0.6 gather_fusion
  97.9 0.2 select_bitcast_fusion.2
  98.2 0.1 reshape_reshape.7
  98.4 0.1 squeeze.10
  98.5 0.1 reshape_reshape.8
  98.7 0.0 copy-start.2
  98.7 0.7 multiply_reduce_fusion
  99.4 0.2 copy-done.2
  99.6 0.5 fusion.6
  100.1 0.5 fusion.7
  100.6 0.7 convolution_bitcast_fusion
  101.3 0.7 fusion
  102.0 0.9 fusion.18
  103.0 0.1 all_to_all.117
  103.1 0.1 copy.66
  103.2 12.2 %all_to_all.132 = bf16[4,128,512]{1,2,0:T(8,128)(2,1)S(1)} all-to-all(bf16[4,128,512]{1,2,0:T(8,128)(2,1)S(1)} %copy.66), channel_id=1, replica_groups=mesh['sect'=2,'seq'=4,'dp'=4] {'seq'}, dimensions={0} | all-to-all | bytes 1048576 | tf_op jit(solution)/shard_map/all_to_all | solution.py:108
  115.4 1.0 copy.67
  (11 shorter events, 0.2 us)
Async XLA Ops:
  0.0 20.7 %copy-start = (bf16[1,8,64,512]{3,2,1,0:T(8,128)(2,1)S(1)}, bf16[1,8,64,512]{3,2,1,0:T(8,128)(2,1)}, u32[]{:S(2)}) copy-start(bf16[1,8,64,512]{3,2,1,0:T(8,128)(2,1)} %param.9) | copy-start | bytes 1572868
  0.0 31.4 %copy-start.1 = (bf16[1,8,64,512]{3,2,1,0:T(8,128)(2,1)S(1)}, bf16[1,8,64,512]{3,2,1,0:T(8,128)(2,1)}, u32[]{:S(2)}) copy-start(bf16[1,8,64,512]{3,2,1,0:T(8,128)(2,1)} %param.10) | copy-start | bytes 1572868
  2.0 10.3 %all-to-all-start.6 = ((bf16[64,4,512]{2,0,1:T(8,128)(2,1)}), bf16[64,4,512]{2,0,1:T(8,128)(2,1)S(1)}, u32[]{:S(2)}, u32[]{:S(2)}) async-start(bf16[64,4,512]{2,0,1:T(8,128)(2,1)} %copy.57), calls=%async_computation.6 | async-start | bytes 524288 | tf_op jit(solution)/shard_map/all_to_all | solution.py:102
  40.5 10.1 %all-to-all-start = ((bf16[1,2,4,64,512]{4,3,2,0,1:T(8,128)(2,1)}), bf16[1,2,4,64,512]{4,3,2,0,1:T(8,128)(2,1)S(1)}, u32[]{:S(2)}, u32[]{:S(2)}) async-start(bf16[1,2,4,64,512]{4,3,2,0,1:T(8,128)(2,1)} %bitcast.1), calls=%async_computation | async-start | bytes 1048576 | tf_op jit(solution)/shard_map/all_to_all | solution.py:81
  50.6 16.1 %all-to-all-start.3 = ((bf16[1,1,4,128,512]{4,3,1,0,2:T(8,128)(2,1)}), bf16[1,1,4,128,512]{4,3,1,0,2:T(8,128)(2,1)S(1)}, u32[]{:S(2)}, u32[]{:S(2)}) async-start(bf16[1,1,4,128,512]{4,3,1,0,2:T(8,128)(2,1)} %bitcast.13), calls=%async_computation.3 | async-start | bytes 1048576 | tf_op jit(solution)/shard_map/all_to_all | solution.py:66
  55.7 30.1 %copy-start.3 = (s32[4]{0:T(128)S(1)}, s32[4]{0:T(128)}, u32[]{:S(2)}) copy-start(s32[4]{0:T(128)} %param.15) | copy-start | bytes 52
  66.7 15.0 %all-to-all-start.5 = ((bf16[1,1,4,128,512]{4,3,1,0,2:T(8,128)(2,1)}), bf16[1,1,4,128,512]{4,3,1,0,2:T(8,128)(2,1)S(1)}, u32[]{:S(2)}, u32[]{:S(2)}) async-start(bf16[1,1,4,128,512]{4,3,1,0,2:T(8,128)(2,1)} %bitcast.21), calls=%async_computation.5 | async-start | bytes 1048576 | tf_op jit(solution)/shard_map/all_to_all | solution.py:73
  81.7 15.6 %all-to-all-start.1 = ((bf16[1,1,4,128,512]{4,3,1,0,2:T(8,128)(2,1)}), bf16[1,1,4,128,512]{4,3,1,0,2:T(8,128)(2,1)S(1)}, u32[]{:S(2)}, u32[]{:S(2)}) async-start(bf16[1,1,4,128,512]{4,3,1,0,2:T(8,128)(2,1)} %bitcast.5), calls=%async_computation.1 | async-start | bytes 1048576 | tf_op jit(solution)/shard_map/all_to_all | solution.py:80
  98.7 1.0 copy-start.2
where the time goes:
time: 117 us; the launch traced here: 116 us
  blocking collectives  40.4 us (35%)
  waiting for transfers between devices  40.1 us (34%)
  starting transfers between devices  19.8 us (17%)
  local copies, waits for them, and re-layouts  10.2 us (9%)
  matrix products  2.8 us (2%)
  other arithmetic  2.19 us (2%)
    all_to_all x1, blocking collectives, shards(): lax.all_to_all(attended_heads, 'seq', split_axis=0, concat_axis=1, tiled=...  12.2 us
    all_to_all x1, blocking collectives, shards(): lax.all_to_all(regroup(query_tiles), 'sect', split_axis=1, concat_axis=3,...  10.7 us
    all_to_all x1, waiting for transfers between devices, shards(): lax.all_to_all(lax.all_to_all(regroup(key_tiles), 'sect', split_axis=1, c...  10.7 us
    all_to_all x1, waiting for transfers between devices, shards(): lax.all_to_all(lax.all_to_all(regroup(query_tiles), 'sect', split_axis=1,...  10.1 us
    all_to_all x1, blocking collectives, shards(): lax.all_to_all(regroup(key_tiles), 'sect', split_axis=1, concat_axis=3, t...  9.08 us
    all_to_all x1, waiting for transfers between devices, shards(): lax.all_to_all(lax.all_to_all(regroup(value_tiles), 'sect', split_axis=1,...  8.71 us
    all_to_all x1, blocking collectives, shards(): lax.all_to_all(text_values[0], 'seq', split_axis=1, concat_axis=0, tiled=...  8.41 us
    all_to_all x1, waiting for transfers between devices, shards(): lax.all_to_all(regroup(value_tiles), 'sect', split_axis=1, concat_axis=3,...  5.72 us
  transfers between devices with their start and end apart: 5, of which 5 were waited for; matrix products, arithmetic and copies ran while one was open for 5% of the time, Pallas kernels for 0%

commit v1 on v0

--- a/solution.py
+++ b/solution.py
@@ -5,6 +5,22 @@
 from jax.sharding import PartitionSpec as P
 
 HD = 128
+
+
+def exchange_in_pairs(shard, axis, split, join):
+    ways, here = (lax.axis_size(axis), lax.axis_index(axis))
+    width = shard.shape[split] // ways
+    shape = list(shard.shape)
+    shape[split] = width
+    height = shape[join]
+    shape[join] = height * ways
+    full = jnp.zeros(shape, shard.dtype)
+    for mask in range(ways):
+        part = lax.dynamic_slice_in_dim(shard, (here ^ mask) * width, width, axis=split)
+        if mask:
+            part = lax.ppermute(part, axis, [(d, d ^ mask) for d in range(ways)])
+        full = lax.dynamic_update_slice_in_dim(full, part, (here ^ mask) * height, axis=join)
+    return full
 
 
 def attend(queries_flat, keys_video, values_video, keys_text, values_text, length):
@@ -100,7 +116,7 @@
     video_values = arrange(relayed[2])
     keys_text, values_text = (
         lax.all_to_all(text_keys[0], "seq", split_axis=1, concat_axis=0, tiled=True),
-        lax.all_to_all(text_values[0], "seq", split_axis=1, concat_axis=0, tiled=True),
+        exchange_in_pairs(text_values[0], "seq", 1, 0),
     )
     attended_heads = attend(
         video_queries, video_keys, video_values, keys_text, values_text, text_lengths[0]

time: 117 us -> 111 us (0.949)
  waiting for transfers between devices: 40.1 us -> 29.8 us
  blocking collectives: 40.4 us -> 43.1 us
  matrix products: 2.8 us -> 4.99 us
  starting transfers between devices: 19.8 us -> 17.9 us
  local copies, waits for them, and re-layouts: 10.2 us -> 11.8 us
    all_to_all x1, waiting for transfers between devices: 10.7 us -> 2.8 us  [shards(): lax.all_to_all(lax.all_to_all(regroup(key_tiles), 'sect', split_axis=1, c...]
    all_to_all x2 -> x1, waiting for transfers between devices: 10.6 us -> 5.72 us  [shards(): lax.all_to_all(regroup(key_tiles), 'sect', split_axis=1, concat_axis=3, t...]
    all_to_all x2 -> x1, starting transfers between devices: 7.73 us -> 3.49 us  [shards(): lax.all_to_all(regroup(key_tiles), 'sect', split_axis=1, concat_axis=3, t...]
    all_to_all x2, blocking collectives: 17.5 us -> 21.4 us  [the longest x1 11.4 us: shards(): lax.all_to_all(regroup(value_tiles), 'sect', split_axis=1, concat_axis=3,...]
    dynamic_update_slice x0 -> x4, local copies, waits for them, and re-layouts: none -> 2.64 us  [exchange_in_pairs(): lax.dynamic_update_slice_in_dim(full, part, (here ^ mask) * height, axis=...]
    ppermute x0 -> x3, starting transfers between devices: none -> 2.59 us  [exchange_in_pairs(): part = lax.ppermute(part, axis, [(d, d ^ mask) for d in range(ways)])]
    dot_general x1, matrix products: 0.95 us -> 3.1 us  [one_block(): jnp.einsum('hqk,khd->qhd', expo_video.astype(jnp.bfloat16), values_video,...]
    all_to_all x1, starting transfers between devices: 5.14 us -> 3.47 us  [shards(): lax.all_to_all(lax.all_to_all(regroup(query_tiles), 'sect', split_axis=1,...]
  transfers between devices with their start and end apart: 5 -> 7, of which waited for: 5 -> 5; matrix products, arithmetic and copies ran while one was open for 5% -> 7% of each run, Pallas kernels for 0% -> 0%
where the time goes in v1:
time: 111 us
  blocking collectives  43.1 us (39%)
  waiting for transfers between devices  29.8 us (27%)
  starting transfers between devices  17.9 us (16%)
  local copies, waits for them, and re-layouts  11.8 us (11%)
  matrix products  4.99 us (4%)
  other arithmetic  2.26 us (2%)
    all_to_all x1, blocking collectives, shards(): lax.all_to_all(attended_heads, 'seq', split_axis=0, concat_axis=1, tiled=...  12.3 us
    all_to_all x1, blocking collectives, shards(): lax.all_to_all(regroup(value_tiles), 'sect', split_axis=1, concat_axis=3,...  11.4 us
    all_to_all x1, waiting for transfers between devices, shards(): lax.all_to_all(lax.all_to_all(regroup(query_tiles), 'sect', split_axis=1,...  10.8 us
    all_to_all x1, waiting for transfers between devices, shards(): lax.all_to_all(lax.all_to_all(regroup(value_tiles), 'sect', split_axis=1,...  10.3 us
    all_to_all x1, blocking collectives, shards(): lax.all_to_all(text_keys[0], 'seq', split_axis=1, concat_axis=0, tiled=True)  10.1 us
    all_to_all x1, blocking collectives, shards(): lax.all_to_all(regroup(query_tiles), 'sect', split_axis=1, concat_axis=3,...  9.36 us
    all_to_all x1, waiting for transfers between devices, shards(): lax.all_to_all(regroup(key_tiles), 'sect', split_axis=1, concat_axis=3, t...  5.72 us
    all_to_all x1, starting transfers between devices, shards(): lax.all_to_all(lax.all_to_all(regroup(value_tiles), 'sect', split_axis=1,...  4.87 us
  transfers between devices with their start and end apart: 7, of which 5 were waited for; matrix products, arithmetic and copies ran while one was open for 7% of the time, Pallas kernels for 0%

profile of v1, /device:TPU:0, one launch (start us, length us, event | category | flops | bytes accessed | tf_op | source)
XLA Modules:
  0.0 110.9 jit_solution(8525421022184524324)
XLA Ops:
  0.0 1.2 %all_to_all.99 = bf16[64,4,512]{2,1,0:T(4,128)(2,1)S(1)} reshape(bf16[1,64,2048]{2,1,0:T(8,128)(2,1)} %param.12) | data formatting | bytes 524288 | tf_op jit(solution)/shard_map/all_to_all | solution.py:118
  1.3 10.1 %all_to_all.113 = bf16[64,4,512]{2,0,1:T(8,128)(2,1)S(1)} all-to-all(bf16[64,4,512]{2,0,1:T(8,128)(2,1)S(1)} %copy.58), channel_id=1, replica_groups=mesh['sect'=2,'seq'=4,'dp'=4] {'seq'}, dimensions={1} | all-to-all | bytes 524288 | tf_op jit(solution)/shard_map/all_to_all | solution.py:118
  11.3 11.4 %all_to_all.114 = bf16[1,2,4,64,512]{4,3,2,0,1:T(8,128)(2,1)S(1)} all-to-all(bf16[1,2,4,64,512]{4,3,2,0,1:T(8,128)(2,1)} %bitcast.76), channel_id=1, replica_groups=mesh['sect'=2,'seq'=4,'dp'=4] {'sect'}, dimensions={1} | all-to-all | bytes 1048576 | tf_op jit(solution)/shard_map/all_to_all | solution.py:97
  22.7 9.4 %all_to_all.115 = bf16[1,2,4,64,512]{4,3,2,0,1:T(8,128)(2,1)S(1)} all-to-all(bf16[1,2,4,64,512]{4,3,2,0,1:T(8,128)(2,1)S(1)} %bitcast.77), channel_id=1, replica_groups=mesh['sect'=2,'seq'=4,'dp'=4] {'sect'}, dimensions={1} | all-to-all | bytes 1048576 | tf_op jit(solution)/shard_map/all_to_all | solution.py:83
  32.1 3.5 %all-to-all-start.4 = ((bf16[1,2,4,64,512]{4,3,2,0,1:T(8,128)(2,1)}), bf16[1,2,4,64,512]{4,3,2,0,1:T(8,128)(2,1)S(1)}, u32[]{:S(2)}, u32[]{:S(2)}) async-start(bf16[1,2,4,64,512]{4,3,2,0,1:T(8,128)(2,1)} %bitcast.17), calls=%async_computation.4 | async-start | bytes 1048576 | tf_op jit(solution)/shard_map/all_to_all | solution.py:90
  35.6 0.8 copy.45
  36.4 5.7 %all-to-all-done.4 = bf16[1,2,4,64,512]{4,3,2,0,1:T(8,128)(2,1)S(1)} async-done(((bf16[1,2,4,64,512]{4,3,2,0,1:T(8,128)(2,1)}), bf16[1,2,4,64,512]{4,3,2,0,1:T(8,128)(2,1)S(1)}, u32[]{:S(2)}, u32[]{:S(2)}) %all-to-all-start.4) | async-done | bytes 524320 | tf_op jit(solution)/shard_map/all_to_all | solution.py:90
  42.1 4.9 %all-to-all-start.1 = ((bf16[1,1,4,128,512]{4,3,1,0,2:T(8,128)(2,1)}), bf16[1,1,4,128,512]{4,3,1,0,2:T(8,128)(2,1)S(1)}, u32[]{:S(2)}, u32[]{:S(2)}) async-start(bf16[1,1,4,128,512]{4,3,1,0,2:T(8,128)(2,1)} %bitcast.5), calls=%async_computation.1 | async-start | bytes 1048576 | tf_op jit(solution)/shard_map/all_to_all | solution.py:96
  47.0 0.8 copy.49
  47.8 10.3 %all-to-all-done.1 = bf16[1,1,4,128,512]{4,3,1,0,2:T(8,128)(2,1)S(1)} async-done(((bf16[1,1,4,128,512]{4,3,1,0,2:T(8,128)(2,1)}), bf16[1,1,4,128,512]{4,3,1,0,2:T(8,128)(2,1)S(1)}, u32[]{:S(2)}, u32[]{:S(2)}) %all-to-all-start.1) | async-done | bytes 524320 | tf_op jit(solution)/shard_map/all_to_all | solution.py:96
  58.1 3.5 %all-to-all-start.3 = ((bf16[1,1,4,128,512]{4,3,1,0,2:T(8,128)(2,1)}), bf16[1,1,4,128,512]{4,3,1,0,2:T(8,128)(2,1)S(1)}, u32[]{:S(2)}, u32[]{:S(2)}) async-start(bf16[1,1,4,128,512]{4,3,1,0,2:T(8,128)(2,1)} %bitcast.13), calls=%async_computation.3 | async-start | bytes 1048576 | tf_op jit(solution)/shard_map/all_to_all | solution.py:82
  61.6 0.8 copy.53
  62.5 10.8 %all-to-all-done.3 = bf16[1,1,4,128,512]{4,3,1,0,2:T(8,128)(2,1)S(1)} async-done(((bf16[1,1,4,128,512]{4,3,1,0,2:T(8,128)(2,1)}), bf16[1,1,4,128,512]{4,3,1,0,2:T(8,128)(2,1)S(1)}, u32[]{:S(2)}, u32[]{:S(2)}) %all-to-all-start.3) | async-done | bytes 524320 | tf_op jit(solution)/shard_map/all_to_all | solution.py:82
  73.3 3.5 %all-to-all-start.5 = ((bf16[1,1,4,128,512]{4,3,1,0,2:T(8,128)(2,1)}), bf16[1,1,4,128,512]{4,3,1,0,2:T(8,128)(2,1)S(1)}, u32[]{:S(2)}, u32[]{:S(2)}) async-start(bf16[1,1,4,128,512]{4,3,1,0,2:T(8,128)(2,1)} %bitcast.21), calls=%async_computation.5 | async-start | bytes 1048576 | tf_op jit(solution)/shard_map/all_to_all | solution.py:89
  76.8 0.1 collective-permute-start
  76.9 2.4 %collective-permute-start.1 = (bf16[64,512]{1,0:T(8,128)(2,1)S(1)}, bf16[64,512]{1,0:T(8,128)(2,1)S(1)}, u32[]{:S(2)}, u32[]{:S(2)}) collective-permute-start(bf16[64,512]{1,0:T(8,128)(2,1)S(1)} %get-tuple-element.34), channel_id=1, source_target_pairs={{0,8},{4,12},{8,0},{12,4},{1,9},{5,13},{9,1},{13,5},{2,10},{6,14},... | collective-permute-start | bytes 196616 | tf_op jit(solution)/shard_map/ppermute | solution.py:21
  79.3 0.1 collective-permute-start.2
  79.4 0.1 copy.63
  80.2 0.8 sort.17
  81.1 0.5 dynamic_update_slice.15
  81.6 0.1 copy.64
  81.8 0.9 dynamic_update_slice.16
  82.7 0.1 copy.65
  82.8 0.4 dynamic_update_slice.17
  83.2 0.2 collective-permute-done.2
  83.4 0.1 copy.66
  83.5 0.8 dynamic_update_slice.18
  84.4 0.1 reshape.74
  84.4 0.6 copy-done.3
  85.1 0.6 gather_fusion
  85.6 0.6 gather_fusion.1
  86.2 2.8 %all-to-all-done.5 = bf16[1,1,4,128,512]{4,3,1,0,2:T(8,128)(2,1)S(1)} async-done(((bf16[1,1,4,128,512]{4,3,1,0,2:T(8,128)(2,1)}), bf16[1,1,4,128,512]{4,3,1,0,2:T(8,128)(2,1)S(1)}, u32[]{:S(2)}, u32[]{:S(2)}) %all-to-all-start.5) | async-done | bytes 524320 | tf_op jit(solution)/shard_map/all_to_all | solution.py:89
  89.0 0.6 gather_fusion.2
  89.6 0.2 select_bitcast_fusion.2
  89.9 0.1 squeeze.10
  90.1 0.1 reshape_reshape.8
  90.2 0.7 multiply_reduce_fusion
  90.9 0.5 fusion.6
  91.4 0.7 fusion
  92.1 0.7 copy-done
  92.9 0.5 fusion.7
  93.4 0.1 reshape_reshape.7
  93.5 3.1 %fusion.2 = f32[4,128,512]{2,1,0:T(8,128)S(1)} fusion(f32[4,512,512]{1,2,0:T(8,128)} %copy-done, f32[4,512]{1,0:T(4,128)S(1)} %max.8, bf16[512,4,128]{2,1,0:T(4,128)(2,1)S(1)} %reshape_reshape.7), kind=kOutput, calls=%fused_computation.7 | convolution fusion | flops 271581184 | bytes 5775360 | tf_op jit(solution)/shard_map/while/body/eval_jaxpr/hqk,khd->qhd/dot_general | solution.py:53
  96.7 0.7 fusion.11
  97.4 0.1 all_to_all.102
  97.5 0.1 copy.68
  97.6 12.3 %all_to_all.116 = bf16[4,128,512]{1,2,0:T(8,128)(2,1)S(1)} all-to-all(bf16[4,128,512]{1,2,0:T(8,128)(2,1)S(1)} %copy.68), channel_id=1, replica_groups=mesh['sect'=2,'seq'=4,'dp'=4] {'seq'}, dimensions={0} | all-to-all | bytes 1048576 | tf_op jit(solution)/shard_map/all_to_all | solution.py:124
  109.9 1.0 copy.69
  (25 shorter events, 0.3 us)
Async XLA Ops:
  0.0 22.7 %copy-start.1 = (bf16[1,8,64,512]{3,2,1,0:T(8,128)(2,1)S(1)}, bf16[1,8,64,512]{3,2,1,0:T(8,128)(2,1)}, u32[]{:S(2)}) copy-start(bf16[1,8,64,512]{3,2,1,0:T(8,128)(2,1)} %param.9) | copy-start | bytes 1572868
  32.1 10.1 %all-to-all-start.4 = ((bf16[1,2,4,64,512]{4,3,2,0,1:T(8,128)(2,1)}), bf16[1,2,4,64,512]{4,3,2,0,1:T(8,128)(2,1)S(1)}, u32[]{:S(2)}, u32[]{:S(2)}) async-start(bf16[1,2,4,64,512]{4,3,2,0,1:T(8,128)(2,1)} %bitcast.17), calls=%async_computation.4 | async-start | bytes 1048576 | tf_op jit(solution)/shard_map/all_to_all | solution.py:90
  42.1 16.0 %all-to-all-start.1 = ((bf16[1,1,4,128,512]{4,3,1,0,2:T(8,128)(2,1)}), bf16[1,1,4,128,512]{4,3,1,0,2:T(8,128)(2,1)S(1)}, u32[]{:S(2)}, u32[]{:S(2)}) async-start(bf16[1,1,4,128,512]{4,3,1,0,2:T(8,128)(2,1)} %bitcast.5), calls=%async_computation.1 | async-start | bytes 1048576 | tf_op jit(solution)/shard_map/all_to_all | solution.py:96
  47.0 29.8 %copy-start.2 = (bf16[1,64,2048]{2,1,0:T(8,128)(2,1)S(1)}, bf16[1,64,2048]{2,1,0:T(8,128)(2,1)}, u32[]{:S(2)}) copy-start(bf16[1,64,2048]{2,1,0:T(8,128)(2,1)} %param.13) | copy-start | bytes 786436
  47.8 32.4 %copy-start.5 = (s32[4]{0:T(128)S(1)}, s32[4]{0:T(128)}, u32[]{:S(2)}) copy-start(s32[4]{0:T(128)} %param.15) | copy-start | bytes 52
  58.1 15.2 %all-to-all-start.3 = ((bf16[1,1,4,128,512]{4,3,1,0,2:T(8,128)(2,1)}), bf16[1,1,4,128,512]{4,3,1,0,2:T(8,128)(2,1)S(1)}, u32[]{:S(2)}, u32[]{:S(2)}) async-start(bf16[1,1,4,128,512]{4,3,1,0,2:T(8,128)(2,1)} %bitcast.13), calls=%async_computation.3 | async-start | bytes 1048576 | tf_op jit(solution)/shard_map/all_to_all | solution.py:82
  73.3 15.7 %all-to-all-start.5 = ((bf16[1,1,4,128,512]{4,3,1,0,2:T(8,128)(2,1)}), bf16[1,1,4,128,512]{4,3,1,0,2:T(8,128)(2,1)S(1)}, u32[]{:S(2)}, u32[]{:S(2)}) async-start(bf16[1,1,4,128,512]{4,3,1,0,2:T(8,128)(2,1)} %bitcast.21), calls=%async_computation.5 | async-start | bytes 1048576 | tf_op jit(solution)/shard_map/all_to_all | solution.py:89
  76.8 4.8 %collective-permute-start = (bf16[64,512]{1,0:T(8,128)(2,1)S(1)}, bf16[64,512]{1,0:T(8,128)(2,1)S(1)}, u32[]{:S(2)}, u32[]{:S(2)}) collective-permute-start(bf16[64,512]{1,0:T(8,128)(2,1)S(1)} %get-tuple-element.23), channel_id=1, source_target_pairs={{0,4},{4,0},{8,12},{12,8},{1,5},{5,1},{9,13},{13,9},{2,6},{6,2},{1... | collective-permute-start | bytes 196616 | tf_op jit(solution)/shard_map/ppermute | solution.py:21
  76.9 5.8 %collective-permute-start.1 = (bf16[64,512]{1,0:T(8,128)(2,1)S(1)}, bf16[64,512]{1,0:T(8,128)(2,1)S(1)}, u32[]{:S(2)}, u32[]{:S(2)}) collective-permute-start(bf16[64,512]{1,0:T(8,128)(2,1)S(1)} %get-tuple-element.34), channel_id=1, source_target_pairs={{0,8},{4,12},{8,0},{12,4},{1,9},{5,13},{9,1},{13,5},{2,10},{6,14},... | collective-permute-start | bytes 196616 | tf_op jit(solution)/shard_map/ppermute | solution.py:21
  79.3 4.0 %collective-permute-start.2 = (bf16[64,512]{1,0:T(8,128)(2,1)S(1)}, bf16[64,512]{1,0:T(8,128)(2,1)S(1)}, u32[]{:S(2)}, u32[]{:S(2)}) collective-permute-start(bf16[64,512]{1,0:T(8,128)(2,1)S(1)} %get-tuple-element.22), channel_id=1, source_target_pairs={{0,12},{4,8},{8,4},{12,0},{1,13},{5,9},{9,5},{13,1},{2,14},{6,10},... | collective-permute-start | bytes 196616 | tf_op jit(solution)/shard_map/ppermute | solution.py:21
  84.4 0.7 copy-start.3
  90.9 1.9 %copy-start = (f32[4,512,512]{1,2,0:T(8,128)}, f32[4,512,512]{1,2,0:T(8,128)S(1)}, u32[]{:S(2)}) copy-start(f32[4,512,512]{1,2,0:T(8,128)S(1)} %get-tuple-element.40) | copy-start | bytes 12582916
  93.5 3.1 %copy-start.4 = (bf16[256,512]{0,1:T(8,128)(2,1)S(1)}, bf16[256,512]{0,1:T(8,128)(2,1)}, u32[]{:S(2)}) copy-start(bf16[256,512]{0,1:T(8,128)(2,1)} %copy-done.3) | copy-start | bytes 786436
